TPU v7x, 32 devices: a whole 2x2x4 slice. The times are simulated.
32 devices in a mesh: grp: 4 (over y, x), row: 2 (over core), col: 4 (over z).
Axes of the slice: x: 2, y: 2, z: 4, core: 2. Of those that a mesh axis runs over, the one named last changes fastest.
Arguments:
- layer_windows: bfloat16 [4, 768, 16384], P(None, ('row', 'grp', 'col')), may hold values from -0.046875 to 0.046875
- sketches: bfloat16 [4, 16384, 128], P(None, 'col'), may hold values from -6 to 6
- group_of: int32 [4], replicated, may hold values from 0 to 3, each once
Outputs:
- basis: float32 [4, 768, 128], P('grp', ('row', 'col'))
- projection: float32 [4, 128, 16384], P('grp', None, 'col')
Inputs may be any that keep to these rules, and one draw needn't show every extreme that they name: `group_of`: each group audits exactly one matrix.
All inputs are finite; a program needn't handle non-finite values.
Results may differ from a plain program's by a relative error of at most 0.013.
Values may be sent and summed in bfloat16 or wider, within the bound.
A program may use at most 64 MiB of HBM per device.

v0:
```python
import math

import jax
import jax.numpy as jnp
from jax import lax
from jax.sharding import PartitionSpec as P


def across(left, right):
    return lax.dot_general(
        left, right, (((0,), (0,)), ((), ())), preferred_element_type=jnp.float32
    )


def right_solve(lower, power):
    return lax.linalg.triangular_solve(lower, power, left_side=False, lower=True, transpose_a=True)


def per_device(layer_windows, sketches, group_of):
    count = group_of.shape[0]
    slots = jnp.arange(count, dtype=jnp.int32)
    matched = (group_of[None, :] == slots[:, None]).astype(jnp.int32)
    owner_of = jnp.sum(matched * slots[None, :], axis=1)
    ordered = jnp.take(layer_windows, owner_of, axis=0)
    block = lax.all_to_all(
        lax.all_to_all(ordered, "col", split_axis=2, concat_axis=1, tiled=True),
        "grp",
        split_axis=0,
        concat_axis=1,
        tiled=True,
    )[0]
    mine = owner_of[lax.axis_index("grp")]
    omega = lax.dynamic_index_in_dim(sketches, mine, 0, keepdims=False)
    total_rows = block.shape[0] * lax.axis_size("row")
    total_cols = block.shape[1] * lax.axis_size("col")
    share = block.shape[0] // lax.axis_size("col")

    def summed_rows(right):
        return lax.psum(jnp.dot(block, right, preferred_element_type=jnp.float32), "col")

    sketched = summed_rows(omega).astype(jnp.bfloat16)
    back = lax.psum(across(block, sketched).astype(jnp.bfloat16), "row")
    power = summed_rows(back)
    gram = lax.psum(
        jnp.dot(power.T, power, precision=lax.Precision.HIGHEST).astype(jnp.bfloat16), "row"
    ).astype(jnp.float32)
    lower = jnp.linalg.cholesky(gram)
    ortho = right_solve(lower, power) * math.sqrt(total_rows)
    basis_share = lax.dynamic_slice_in_dim(ortho, lax.axis_index("col") * share, share, 0)
    ortho_low = ortho.astype(jnp.bfloat16)
    projected = lax.psum(across(ortho_low, block).astype(jnp.bfloat16), "row").astype(
        jnp.float32
    ) * math.sqrt(total_cols / total_rows)
    return (basis_share[None], projected[None])


def solution(mesh):
    in_specs = (P(None, ("row", "grp", "col"), None), P(None, "col", None), P())
    out_specs = (P("grp", ("row", "col"), None), P("grp", None, "col"))
    return jax.shard_map(
        per_device, mesh=mesh, in_specs=in_specs, out_specs=out_specs, check_vma=False
    )
```

profile of v0, /device:TPU:0, one launch (start us, length us, event | category | flops | bytes accessed | tf_op | source)
XLA Modules:
  0.0 361.0 jit_solution(111216601561720730)
XLA Ops:
  7.2 0.0 copy-start
  7.2 0.9 select_reduce_fusion.1
  8.1 0.9 copy-done
  9.1 2.4 gather_fusion
  11.5 2.3 broadcast_select_fusion
  13.7 15.8 %copy.21 = bf16[4,24,16384]{1,0,2:T(4,128)(2,1)} copy(bf16[4,24,16384]{2,1,0:T(8,128)(2,1)S(1)} %broadcast_select_fusion) | data formatting | bytes 6291456 | tf_op jit(solution)/shard_map/jit(_take)/select_n | solution.py:24
  29.5 24.1 %reshape.44 = bf16[4,2,196608]{2,1,0:T(2,128)(2,1)S(1)} reshape(bf16[16384,4,24]{2,1,0:T(4,128)(2,1)} %bitcast.42) | data formatting | bytes 6291456
  53.7 76.9 %all_to_all.27 = bf16[4,2,196608]{2,1,0:T(2,128)(2,1)} all-to-all(bf16[4,2,196608]{2,1,0:T(2,128)(2,1)S(1)} %reshape.44), channel_id=1, replica_groups=mesh['grp'=4,'row'=2,'col'=4] {'col'}, dimensions={0} | all-to-all | bytes 6291456 | tf_op jit(solution)/shard_map/all_to_all | solution.py:26
  130.6 26.1 %reshape.45 = bf16[16384,4,24]{2,1,0:T(4,128)(2,1)} reshape(bf16[4,2,196608]{2,1,0:T(2,128)(2,1)} %all_to_all.27) | data formatting | bytes 6291456
  156.7 21.4 %copy.23 = bf16[4,4,24,4096]{3,2,1,0:T(8,128)(2,1)} copy(bf16[4,4,24,4096]{2,0,3,1:T(4,128)(2,1)} %bitcast.43) | data formatting | bytes 6291456 | tf_op jit(solution)/shard_map/all_to_all | solution.py:26
  178.1 3.7 %all-to-all-start.1 = ((bf16[4,96,4096]{2,1,0:T(8,128)(2,1)}), bf16[4,96,4096]{2,1,0:T(8,128)(2,1)S(1)}, u32[]{:S(2)}, u32[]{:S(2)}) async-start(bf16[4,96,4096]{2,1,0:T(8,128)(2,1)} %bitcast.44), calls=%async_computation.1 | async-start | bytes 6291456 | tf_op jit(solution)/shard_map/all_to_all | solution.py:25
  181.8 0.2 all-reduce.5.cloned.1.call-start
  182.0 0.6 dynamic_slice.10
  184.6 32.5 %all-to-all-done.1 = bf16[4,96,4096]{2,1,0:T(8,128)(2,1)S(1)} async-done(((bf16[4,96,4096]{2,1,0:T(8,128)(2,1)}), bf16[4,96,4096]{2,1,0:T(8,128)(2,1)S(1)}, u32[]{:S(2)}, u32[]{:S(2)}) %all-to-all-start.1) | async-done | bytes 3145760 | tf_op jit(solution)/shard_map/all_to_all | solution.py:25
  217.1 0.0 copy-start.2
  217.1 3.0 fusion
  220.0 21.1 %all-reduce.10 = bf16[384,128]{1,0:T(8,128)(2,1)S(1)} all-reduce(f32[384,128]{1,0:T(8,128)S(1)} %fusion), channel_id=1, replica_groups=mesh['grp'=4,'row'=2,'col'=4] {'col'}, use_global_device_ids=true, to_apply=%region_1.2 | all-reduce | flops 49152 | bytes 294912 | tf_op jit(solution)/shard_map/psum | solution.py:39
  241.1 2.0 convolution_convert_fusion.1
  243.1 0.0 all-reduce.5.cloned.1.call-update
  243.2 0.0 all-reduce.7.cloned.1.call-start
  243.2 17.1 %all-reduce.5.cloned.1.call-done = bf16[4096,128]{1,0:T(8,128)(2,1)} async-done(((bf16[4096,128]{1,0:T(8,128)(2,1)}), bf16[4096,128]{1,0:T(8,128)(2,1)}) %all-reduce.5.cloned.1.call-update) | async-done | bytes 1048592 | tf_op jit(solution)/shard_map/psum | solution.py:42
  260.3 0.0 copy-done.2
  260.3 2.9 fusion.10
  263.2 0.0 all-reduce.7.cloned.1.call-update
  263.2 0.0 all-reduce.9.cloned.1.call-start
  263.2 36.3 %all-reduce.7.cloned.1.call-done = f32[384,128]{1,0:T(8,128)} async-done(((f32[384,128]{1,0:T(8,128)}), f32[384,128]{1,0:T(8,128)}) %all-reduce.7.cloned.1.call-update) | async-done | bytes 196624 | tf_op jit(solution)/shard_map/psum | solution.py:39
  299.5 1.5 convolution_convert_fusion.2
  301.0 3.4 psum.38
  304.5 0.1 copy.25
  304.6 11.7 %cholesky.16 = f32[128,128]{1,0:T(8,128)S(1)} custom-call(f32[128,128]{1,0:T(8,128)S(1)} %fusion.7), custom_call_target="Cholesky" | custom-call | tf_op jit(solution)/shard_map/jit(cholesky)/cholesky | solution.py:47
  316.3 0.6 compare_reduce_fusion
  317.0 0.7 fusion.5
  317.6 9.8 %custom-call.6 = f32[1,128,128]{1,2,0:T(8,128)S(1)} custom-call(f32[1,128,128]{2,1,0:T(8,128)S(1)} %fusion.5), custom_call_target="InvertDiagBlocksLowerTriangular" | custom-call | tf_op jit(solution)/shard_map/triangular_solve | solution.py:16
  327.5 1.2 convolution_multiply_fusion
  328.7 0.0 copy-start.1
  328.7 3.8 %convolution_convert_fusion = bf16[128,4096]{1,0:T(8,128)(2,1)} fusion(bf16[384,4096]{1,0:T(8,128)(2,1)} %bitcast.41, f32[384,128]{1,0:T(8,128)S(1)} %convolution_multiply_fusion), kind=kOutput, calls=%fused_computation.1 | convolution fusion | flops 403226624 | bytes 4390912 | tf_op jit(solution)/shard_map/dot_general | solution.py:10
  332.5 0.0 all-reduce.9.cloned.1.call-update
  332.5 0.6 dynamic-slice_bitcast_fusion
  333.1 18.6 %all-reduce.9.cloned.1.call-done = bf16[128,4096]{1,0:T(8,128)(2,1)} async-done(((bf16[128,4096]{1,0:T(8,128)(2,1)}), bf16[128,4096]{1,0:T(8,128)(2,1)}) %all-reduce.9.cloned.1.call-update) | async-done | bytes 1048592 | tf_op jit(solution)/shard_map/psum | solution.py:51
  351.7 2.8 multiply_bitcast_fusion
  354.5 0.0 copy-done.1
  (5 shorter events, 0.1 us)
Async XLA Ops:
  7.2 1.9 copy-start
  178.1 39.0 %all-to-all-start.1 = ((bf16[4,96,4096]{2,1,0:T(8,128)(2,1)}), bf16[4,96,4096]{2,1,0:T(8,128)(2,1)S(1)}, u32[]{:S(2)}, u32[]{:S(2)}) async-start(bf16[4,96,4096]{2,1,0:T(8,128)(2,1)} %bitcast.44), calls=%async_computation.1 | async-start | bytes 6291456 | tf_op jit(solution)/shard_map/all_to_all | solution.py:25
  181.8 78.5 %all-reduce.5.cloned.1.call-start = ((), (), s32[]{:S(2)}) async-start(), calls=%async_computation.2 | async-start | bytes 2097152 | tf_op jit(solution)/shard_map/psum | solution.py:42
  217.1 43.2 %copy-start.2 = (bf16[4,96,4096]{2,1,0:T(8,128)(2,1)}, bf16[4,96,4096]{2,1,0:T(8,128)(2,1)S(1)}, u32[]{:S(2)}) copy-start(bf16[4,96,4096]{2,1,0:T(8,128)(2,1)S(1)} %all-to-all-done.1) | copy-start | bytes 9437188
  243.2 56.4 %all-reduce.7.cloned.1.call-start = ((), (), s32[]{:S(2)}) async-start(), calls=%async_computation.3 | async-start | bytes 393216 | tf_op jit(solution)/shard_map/psum | solution.py:39
  263.2 88.5 %all-reduce.9.cloned.1.call-start = ((), (), s32[]{:S(2)}) async-start(), calls=%async_computation.4 | async-start | bytes 2097152 | tf_op jit(solution)/shard_map/psum | solution.py:51
  328.7 25.8 %copy-start.1 = (bf16[4,24,16384]{2,1,0:T(8,128)(2,1)S(1)}, bf16[4,24,16384]{2,1,0:T(8,128)(2,1)}, u32[]{:S(2)}) copy-start(bf16[4,24,16384]{2,1,0:T(8,128)(2,1)} %param.3) | copy-start | bytes 9437188
Sparse Core Ops, SparseCore 0:
  243.3 16.9 all-reduce.4
  263.3 36.1 all-reduce.6
  332.6 19.0 all-reduce.8
where the time goes:
time: 362 us; the launch traced here: 361 us
  waiting for transfers between devices  105 us (29%)
  blocking collectives  101 us (28%)
  local copies, waits for them, and re-layouts  92.1 us (25%)
  other arithmetic  28.8 us (8%)
  between operations  15.8 us (4%)
  matrix products  14.3 us (4%)
  starting transfers between devices  4.01 us (1%)
    all_to_all x1, blocking collectives, per_device(): lax.all_to_all(ordered, 'col', split_axis=2, concat_axis=1, tiled=True)  76.9 us
    unnamed x8, local copies, waits for them, and re-layouts  51.2 us
    psum x1, waiting for transfers between devices, summed_rows(): lax.psum(jnp.dot(block, right, preferred_element_type=jnp.float32), 'col')  36.3 us
    all_to_all x1, waiting for transfers between devices, per_device(): lax.all_to_all(lax.all_to_all(ordered, 'col', split_axis=2, concat_axis=1...  32.5 us
    all_to_all x1, local copies, waits for them, and re-layouts, per_device(): lax.all_to_all(ordered, 'col', split_axis=2, concat_axis=1, tiled=True)  21.4 us
    psum x1, blocking collectives, summed_rows(): lax.psum(jnp.dot(block, right, preferred_element_type=jnp.float32), 'col')  21.1 us
    psum x1, waiting for transfers between devices, per_device(): lax.psum(across(ortho_low, block).astype(jnp.bfloat16), 'row')  18.6 us
    psum x1, waiting for transfers between devices, per_device(): back = lax.psum(across(block, sketched).astype(jnp.bfloat16), 'row')  17.1 us
  transfers between devices with their start and end apart: 4, of which 4 were waited for; matrix products, arithmetic and copies ran while one was open for 0% of the time, Pallas kernels for 0%

commit v1 on v0

--- a/solution.py
+++ b/solution.py
@@ -1,9 +1,16 @@
+import functools
 import math
 
 import jax
 import jax.numpy as jnp
 from jax import lax
+from jax.experimental import pallas as pl
+from jax.experimental.pallas import tpu as pltpu
 from jax.sharding import PartitionSpec as P
+
+MESH = pl.DeviceIdType.MESH
+F32 = jnp.float32
+BF16 = jnp.bfloat16
 
 
 def across(left, right):
@@ -16,11 +23,15 @@
     return lax.linalg.triangular_solve(lower, power, left_side=False, lower=True, transpose_a=True)
 
 
-def per_device(layer_windows, sketches, group_of):
+def owners(group_of):
     count = group_of.shape[0]
     slots = jnp.arange(count, dtype=jnp.int32)
     matched = (group_of[None, :] == slots[:, None]).astype(jnp.int32)
-    owner_of = jnp.sum(matched * slots[None, :], axis=1)
+    return jnp.sum(matched * slots[None, :], axis=1)
+
+
+def per_device(layer_windows, sketches, group_of):
+    owner_of = owners(group_of)
     ordered = jnp.take(layer_windows, owner_of, axis=0)
     block = lax.all_to_all(
         lax.all_to_all(ordered, "col", split_axis=2, concat_axis=1, tiled=True),
@@ -54,9 +65,220 @@
     return (basis_share[None], projected[None])
 
 
+def range_kernel(groups, zs, chunks, ordered, omega, block, power, gram,
+                 part1, part2, rs1, rs2, sk, bt, bt_in, back, gpart, g_in,
+                 a_send, a_recv, own_sem, s1_send, s1_recv, g1_send, g1_recv,
+                 b_send, b_recv, s2_send, s2_recv, g2_send, g2_recv, x_send, x_recv):
+    g, r, c = lax.axis_index("grp"), lax.axis_index("row"), lax.axis_index("col")
+    height = ordered.shape[1]
+    wide = block.shape[1]
+    share = block.shape[0] // zs
+    other = (g, 1 - r, c)
+
+    def partner(dz):
+        if zs != 4 or dz == 2:
+            return lax.rem(c + dz, zs)
+        return (c, c + 1 - 2 * lax.rem(c, 2), None, 3 - c)[dz]
+
+    order = (2, 3, 1) if zs == 4 else tuple(range(1, zs))
+
+    barrier = pltpu.get_barrier_semaphore()
+    for dz in range(zs):
+        for dg in range(groups):
+            if dz or dg:
+                to = (lax.rem(g + dg, groups), r, partner(dz))
+                pl.semaphore_signal(barrier, inc=1, device_id=to, device_id_type=MESH)
+    pl.semaphore_signal(barrier, inc=1, device_id=other, device_id_type=MESH)
+    pl.semaphore_wait(barrier, groups * zs)
+
+    def spot(gi, ci):
+        return block.at[pl.ds(pl.multiple_of((gi * zs + ci) * height, 8), height), :]
+
+    def cut(gi, ci):
+        return ordered.at[gi, :, pl.ds(pl.multiple_of(ci * wide, 128), wide)]
+
+    sends = []
+    for dz in order + (0,):
+        for dg in range(groups):
+            tg, tc = lax.rem(g + dg, groups), partner(dz)
+            if dz or dg:
+                copy = pltpu.make_async_remote_copy(
+                    src_ref=cut(tg, tc), dst_ref=spot(g, c),
+                    send_sem=a_send.at[dz * groups + dg], recv_sem=a_recv.at[dz * groups + dg],
+                    device_id=(tg, r, tc), device_id_type=MESH)
+                copy.start()
+                sends.append(copy)
+    own = pltpu.make_async_copy(cut(g, c), spot(g, c), own_sem)
+    own.start()
+    own.wait()
+    for copy in sends:
+        copy.wait()
+
+    def rows(k):
+        return pl.ds(pl.multiple_of(k * share, 16), share)
+
+    def scatter(compute, part, rs, send_sem, recv_sem):
+        copies = []
+        for dz in order:
+            k = partner(dz)
+            part[dz] = compute(block[rows(k), :])
+            copy = pltpu.make_async_remote_copy(
+                src_ref=part.at[dz], dst_ref=rs.at[dz],
+                send_sem=send_sem.at[dz], recv_sem=recv_sem.at[dz],
+                device_id=(g, r, k), device_id_type=MESH)
+            copy.start()
+            copies.append(copy)
+        total = compute(block[rows(c), :])
+        for copy in copies:
+            copy.wait()
+        for dz in range(1, zs):
+            total = total + rs[dz]
+        return total
+
+    def gather(ref, send_sem, recv_sem):
+        copies = []
+        for dz in order:
+            copy = pltpu.make_async_remote_copy(
+                src_ref=ref.at[rows(c), :], dst_ref=ref.at[rows(c), :],
+                send_sem=send_sem.at[dz], recv_sem=recv_sem.at[dz],
+                device_id=(g, r, partner(dz)), device_id_type=MESH)
+            copy.start()
+            copies.append(copy)
+        for copy in copies:
+            copy.wait()
+
+    sk[rows(c), :] = scatter(
+        lambda a: jnp.dot(a, omega[...], preferred_element_type=F32),
+        part1, rs1, s1_send, s1_recv).astype(BF16)
+    gather(sk, g1_send, g1_recv)
+
+    turned = sk[...].astype(F32).T.astype(BF16)
+    step = wide // chunks
+    copies = []
+    for i in range(chunks):
+        bt[i] = jnp.dot(turned, block[:, i * step:(i + 1) * step],
+                        preferred_element_type=F32).astype(BF16)
+        copy = pltpu.make_async_remote_copy(
+            src_ref=bt.at[i], dst_ref=bt_in.at[i], send_sem=b_send.at[i], recv_sem=b_recv.at[i],
+            device_id=other, device_id_type=MESH)
+        copy.start()
+        copies.append(copy)
+    for i in range(chunks):
+        copies[i].wait()
+        back[:, i * step:(i + 1) * step] = (bt[i].astype(F32) + bt_in[i].astype(F32)).astype(BF16)
+
+    power[rows(c), :] = scatter(
+        lambda a: lax.dot_general(a, back[...], (((1,), (1,)), ((), ())),
+                                  preferred_element_type=F32),
+        part2, rs2, s2_send, s2_recv)
+    gather(power, g2_send, g2_recv)
+
+    whole = power[...]
+    gpart[...] = jnp.dot(whole.T, whole, precision=lax.Precision.HIGHEST,
+                         preferred_element_type=F32)
+    copy = pltpu.make_async_remote_copy(
+        src_ref=gpart, dst_ref=g_in, send_sem=x_send, recv_sem=x_recv,
+        device_id=other, device_id_type=MESH)
+    copy.start()
+    copy.wait()
+    gram[...] = gpart[...] + g_in[...]
+
+
+def project_kernel(chunks, turned, block, out, mine, theirs, send_sem, recv_sem):
+    other = (lax.axis_index("grp"), 1 - lax.axis_index("row"), lax.axis_index("col"))
+    barrier = pltpu.get_barrier_semaphore()
+    pl.semaphore_signal(barrier, inc=1, device_id=other, device_id_type=MESH)
+    pl.semaphore_wait(barrier, 1)
+    step = block.shape[1] // chunks
+    copies = []
+    for i in range(chunks):
+        mine[i] = jnp.dot(turned[...], block[:, i * step:(i + 1) * step],
+                          preferred_element_type=F32).astype(BF16)
+        copy = pltpu.make_async_remote_copy(
+            src_ref=mine.at[i], dst_ref=theirs.at[i],
+            send_sem=send_sem.at[i], recv_sem=recv_sem.at[i],
+            device_id=other, device_id_type=MESH)
+        copy.start()
+        copies.append(copy)
+    for i in range(chunks):
+        copies[i].wait()
+        out[:, i * step:(i + 1) * step] = mine[i].astype(F32) + theirs[i].astype(F32)
+
+
+def fused_device(groups, zs, layer_windows, sketches, group_of):
+    owner_of = owners(group_of)
+    count, height, total_cols = layer_windows.shape
+    rank = sketches.shape[2]
+    wide = total_cols // zs
+    deep = height * groups * zs
+    share = deep // zs
+    total_rows = deep * 2
+    chunks = 4
+    step = wide // chunks
+    ordered = layer_windows.at[owner_of].get(mode="promise_in_bounds", unique_indices=True)
+    mine = owner_of[lax.axis_index("grp")]
+    omega = lax.dynamic_index_in_dim(sketches, mine, 0, keepdims=False)
+    vmem = pl.BlockSpec(memory_space=pltpu.VMEM)
+    dma = pltpu.SemaphoreType.DMA
+    block, power, gram = pl.pallas_call(
+        functools.partial(range_kernel, groups, zs, chunks),
+        out_shape=(
+            jax.ShapeDtypeStruct((deep, wide), BF16),
+            jax.ShapeDtypeStruct((deep, rank), F32),
+            jax.ShapeDtypeStruct((rank, rank), F32),
+        ),
+        in_specs=[pl.BlockSpec(memory_space=pl.ANY), vmem],
+        out_specs=(vmem, vmem, vmem),
+        scratch_shapes=[
+            pltpu.VMEM((zs, share, rank), F32),
+            pltpu.VMEM((zs, share, rank), F32),
+            pltpu.VMEM((zs, share, rank), F32),
+            pltpu.VMEM((zs, share, rank), F32),
+            pltpu.VMEM((deep, rank), BF16),
+            pltpu.VMEM((chunks, rank, step), BF16),
+            pltpu.VMEM((chunks, rank, step), BF16),
+            pltpu.VMEM((rank, wide), BF16),
+            pltpu.VMEM((rank, rank), F32),
+            pltpu.VMEM((rank, rank), F32),
+            dma((zs * groups,)), dma((zs * groups,)), dma,
+            dma((zs,)), dma((zs,)), dma((zs,)), dma((zs,)),
+            dma((chunks,)), dma((chunks,)),
+            dma((zs,)), dma((zs,)), dma((zs,)), dma((zs,)),
+            dma, dma,
+        ],
+        compiler_params=pltpu.CompilerParams(collective_id=0, has_side_effects=True),
+        name="range_finder",
+    )(ordered, omega)
+    lower = jnp.linalg.cholesky(gram)
+    ortho = right_solve(lower, power) * math.sqrt(total_rows)
+    basis_share = lax.dynamic_slice_in_dim(ortho, lax.axis_index("col") * share, share, 0)
+    turned = ortho.astype(BF16).T
+    projected = pl.pallas_call(
+        functools.partial(project_kernel, chunks),
+        out_shape=jax.ShapeDtypeStruct((rank, wide), F32),
+        in_specs=[vmem, vmem],
+        out_specs=vmem,
+        scratch_shapes=[
+            pltpu.VMEM((chunks, rank, step), BF16),
+            pltpu.VMEM((chunks, rank, step), BF16),
+            dma((chunks,)), dma((chunks,)),
+        ],
+        compiler_params=pltpu.CompilerParams(collective_id=1, has_side_effects=True),
+        name="projector",
+    )(turned, block)
+    return (basis_share[None], (projected * math.sqrt(total_cols / total_rows))[None])
+
+
 def solution(mesh):
     in_specs = (P(None, ("row", "grp", "col"), None), P(None, "col", None), P())
     out_specs = (P("grp", ("row", "col"), None), P("grp", None, "col"))
-    return jax.shard_map(
-        per_device, mesh=mesh, in_specs=in_specs, out_specs=out_specs, check_vma=False
-    )
+    groups, halves, zs = mesh.shape["grp"], mesh.shape["row"], mesh.shape["col"]
+
+    def body(layer_windows, sketches, group_of):
+        height = layer_windows.shape[1]
+        fits = halves == 2 and height % 8 == 0 and (height * groups) % 16 == 0
+        if fits and groups == layer_windows.shape[0] and layer_windows.shape[2] % (zs * 512) == 0:
+            return fused_device(groups, zs, layer_windows, sketches, group_of)
+        return per_device(layer_windows, sketches, group_of)
+
+    return jax.shard_map(body, mesh=mesh, in_specs=in_specs, out_specs=out_specs, check_vma=False)

time: 362 us -> 153 us (0.42)
  Pallas kernels: 0 us -> 113 us
  waiting for transfers between devices: 105 us -> 0 us
  blocking collectives: 101 us -> 0 us
  local copies, waits for them, and re-layouts: 92.1 us -> 7.04 us
  between operations: 15.8 us -> 2.66 us
  matrix products: 14.3 us -> 1.33 us
  starting transfers between devices: 4.01 us -> 0 us
    pallas_call x0 -> x2, Pallas kernels: none -> 113 us  [the longest x1 106 us: fused_device(): pl.pallas_call(functools.partial(range_kernel, groups, zs, chunks), out_s...]
    all_to_all x1 -> x0, blocking collectives: 76.9 us -> none  [per_device(): lax.all_to_all(ordered, 'col', split_axis=2, concat_axis=1, tiled=True)]
    psum x3 -> x0, waiting for transfers between devices: 72 us -> none  [the longest x1 36.3 us: summed_rows(): lax.psum(jnp.dot(block, right, preferred_element_type=jnp.float32), 'col')]
    unnamed x8 -> x2, local copies, waits for them, and re-layouts: 51.2 us -> 0.01 us
    all_to_all x1 -> x0, waiting for transfers between devices: 32.5 us -> none  [per_device(): lax.all_to_all(lax.all_to_all(ordered, 'col', split_axis=2, concat_axis=1...]
    psum x2 -> x0, blocking collectives: 24.5 us -> none  [the longest x1 21.1 us: summed_rows(): lax.psum(jnp.dot(block, right, preferred_element_type=jnp.float32), 'col')]
    all_to_all x1 -> x0, local copies, waits for them, and re-layouts: 21.4 us -> none  [per_device(): lax.all_to_all(ordered, 'col', split_axis=2, concat_axis=1, tiled=True)]
    select_n x1 -> x0, local copies, waits for them, and re-layouts: 15.8 us -> none  [per_device(): ordered = jnp.take(layer_windows, owner_of, axis=0)]
  transfers between devices with their start and end apart: 4 -> 0, of which waited for: 4 -> 0; matrix products, arithmetic and copies ran while one was open for 0% -> 0% of each run, Pallas kernels for 0% -> 0%
where the time goes in v1:
time: 153 us; the launch traced here: 152 us
  Pallas kernels  113 us (74%)
  other arithmetic  28.4 us (19%)
  local copies, waits for them, and re-layouts  7.04 us (5%)
  between operations  2.66 us (2%)
    pallas_call x1, Pallas kernels, fused_device(): pl.pallas_call(functools.partial(range_kernel, groups, zs, chunks), out_s...  106 us
    another operation x3, other arithmetic, fused_device(): lower = jnp.linalg.cholesky(gram)  12.4 us
    another operation x2, other arithmetic, right_solve(): lax.linalg.triangular_solve(lower, power, left_side=False, lower=True, tr...  10.5 us
    pallas_call x1, Pallas kernels, fused_device(): pl.pallas_call(functools.partial(project_kernel, chunks), out_shape=jax.S...  6.41 us
    broadcast_in_dim x1, other arithmetic, fused_device(): (projected * math.sqrt(total_cols / total_rows))[None]  3.12 us

profile of v1, /device:TPU:0, one launch (start us, length us, event | category | flops | bytes accessed | tf_op | source)
XLA Modules:
  0.0 152.3 jit_solution(7262926154524334629)
XLA Ops:
  0.6 0.0 copy-start
  0.6 0.9 select_reduce_fusion.1
  1.6 0.6 dynamic_slice.10
  4.1 2.3 %dynamic-slice_bitcast_fusion.omega = bf16[4096,128]{1,0:T(8,128)(2,1)} fusion(bf16[4,4096,128]{2,1,0:T(8,128)(2,1)} %param.4, s32[]{:T(128)S(6)} %select_n.26), kind=kLoop, calls=%fused_computation.3 | loop fusion | bytes 2097156 | tf_op jit(solution)/shard_map/jit(dynamic_index_in_dim)/squeeze | solution.py:220
  6.4 0.0 copy-done
  6.4 2.4 %gather_fusion = bf16[4,24,16384]{2,1,0:T(8,128)(2,1)} fusion(bf16[4,24,16384]{2,1,0:T(8,128)(2,1)S(1)} %copy-done, s32[1024]{0:T(1024)S(1)} %pad_clamp_fusion), kind=kCustom, calls=%fused_computation | custom fusion | bytes 6291472 | tf_op jit(solution)/shard_map/gather | solution.py:218
  8.8 106.4 %range_finder.1 = (bf16[384,4096]{1,0:T(8,128)(2,1)}, f32[384,128]{1,0:T(8,128)}, f32[128,128]{1,0:T(8,128)}) custom-call(bf16[4,24,16384]{2,1,0:T(8,128)(2,1)} %gather_fusion, bf16[4096,128]{1,0:T(8,128)(2,1)} %dynamic-slice_bitcast_fusion.omega), custom_call_target="tpu_custom_call" | custom-call | tf_op jit(solution)/shard_map/range_finder/pallas_call | solution.py:223
  115.3 0.9 copy.10
  116.2 0.9 fusion.2
  117.1 11.7 %cholesky.16 = f32[128,128]{1,0:T(8,128)S(1)} custom-call(f32[128,128]{1,0:T(8,128)S(1)} %fusion.2), custom_call_target="Cholesky" | custom-call | tf_op jit(solution)/shard_map/jit(cholesky)/cholesky | solution.py:252
  128.8 0.6 compare_reduce_fusion
  129.5 0.7 fusion
  130.1 9.8 %custom-call.6 = f32[1,128,128]{1,2,0:T(8,128)S(1)} custom-call(f32[1,128,128]{2,1,0:T(8,128)S(1)} %fusion), custom_call_target="InvertDiagBlocksLowerTriangular" | custom-call | tf_op jit(solution)/shard_map/triangular_solve | solution.py:23
  140.0 1.3 convolution_multiply_fusion
  141.3 0.1 constant_dynamic-slice_fusion
  141.4 0.7 convert_bitcast_fusion.turned
  142.1 6.4 %projector.1 = f32[128,4096]{1,0:T(8,128)} custom-call(bf16[128,384]{1,0:T(8,128)(2,1)} %convert_bitcast_fusion.turned, bf16[384,4096]{1,0:T(8,128)(2,1)} %get-tuple-element.7.block), custom_call_target="tpu_custom_call" | custom-call | tf_op jit(solution)/shard_map/projector/pallas_call | solution.py:256
  148.5 0.7 copy.12
  149.2 3.1 %multiply_bitcast_fusion = f32[1,128,4096]{2,1,0:T(8,128)} fusion(f32[128,4096]{1,0:T(8,128)} %projector.1), kind=kLoop, calls=%fused_computation.1 | loop fusion | flops 524288 | bytes 4194304 | tf_op jit(solution)/shard_map/broadcast_in_dim | solution.py:269
  (3 shorter events, 0.0 us)
Async XLA Ops:
  0.6 5.8 %copy-start = (bf16[4,24,16384]{2,1,0:T(8,128)(2,1)S(1)}, bf16[4,24,16384]{2,1,0:T(8,128)(2,1)}, u32[]{:S(2)}) copy-start(bf16[4,24,16384]{2,1,0:T(8,128)(2,1)} %param.3) | copy-start | bytes 9437188
